TPU v7x, 256 devices: a whole 4x4x8 slice. The times are simulated.
256 devices in a mesh: tok: 8 (over z), tp: 16 (over y, x), grp: 2 (over core).
Axes of the slice: x: 4, y: 4, z: 8, core: 2. Of those that a mesh axis runs over, the one named last changes fastest.
Arguments:
- hidden: bfloat16 [2048, 6144], P(('tok', 'grp'), 'tp'), may hold values from -6 to 6
- gain: bfloat16 [6144], P('tp'), may hold values from 0.5 to 1.5
- expert_ids: int32 [2048, 2], P(('tok', 'grp')), may hold values from 0 to 7, all different within a row; in each aligned block of 128 rows (0 to 127, 128 to 255, ...) at most 40 rows name the same one
- gate_weights: float32 [2048, 2], P(('tok', 'grp')), may hold values from 0.1 to 0.9
- segment_ids: int32 [2048], P(('tok', 'grp')), may hold values from 0 to 15, never falling along the last dimension, each value on 1 to 384 neighbouring positions
- upstream: bfloat16 [2048, 6144], P(('tok', 'grp'), 'tp'), may hold values from -6 to 6
- w_gate: bfloat16 [8, 6144, 8192], P('tok', None, ('tp', 'grp')), may hold values from -0.078125 to 0.078125
- w_up: bfloat16 [8, 6144, 8192], P('tok', None, ('tp', 'grp')), may hold values from -0.078125 to 0.078125
- w_down: bfloat16 [8, 8192, 6144], P('tok', ('tp', 'grp')), may hold values from -0.0625 to 0.0625
Outputs:
- mixed: bfloat16 [2048, 6144], P(('tok', 'grp'), 'tp')
- importance: float32 [8, 8192], P('tok', ('tp', 'grp'))
Inputs may be any that keep to these rules, and one draw needn't show every extreme that they name: `expert_ids`: each token names 2 different experts. Within the tokens of one token shard (aligned blocks of 128 rows) no expert is named by more than 40 tokens, and in some block one expert is named by exactly 40. `segment_ids`: never falling along the tokens; every document holds between 1 and 384 tokens.
All inputs are finite; a program needn't handle non-finite values.
Results may differ from a plain program's by a relative error of at most 0.0095.
Values may be sent and summed in bfloat16 or wider, within the bound.
No kernel may reach another device: no remote copies, remote signals or barrier semaphores. Data moves between devices by JAX's collectives and lax.ppermute only.
A program may use at most 128 MiB of HBM per device.

v0:
```python
import jax
import jax.numpy as jnp
from jax import lax
from jax.sharding import PartitionSpec as P


def expert_pass(rows_in, cot_in, gate_mat, up_mat, down_mat):
    gate_pre = jnp.dot(rows_in, gate_mat, preferred_element_type=jnp.float32)
    up_proj = jnp.dot(rows_in, up_mat, preferred_element_type=jnp.float32)
    sigmoid_gate = jax.nn.sigmoid(gate_pre)
    activated = gate_pre * sigmoid_gate
    hidden_act = (activated * up_proj).astype(jnp.bfloat16)
    grad_act = lax.dot_general(
        cot_in, down_mat, (((1,), (1,)), ((), ())), preferred_element_type=jnp.float32
    )
    grad_gate = (
        grad_act * up_proj * sigmoid_gate * (1.0 + gate_pre * (1.0 - sigmoid_gate))
    ).astype(jnp.bfloat16)
    grad_up = (grad_act * activated).astype(jnp.bfloat16)
    grad_wgate = lax.dot_general(
        rows_in, grad_gate, (((0,), (0,)), ((), ())), preferred_element_type=jnp.float32
    )
    grad_wup = lax.dot_general(
        rows_in, grad_up, (((0,), (0,)), ((), ())), preferred_element_type=jnp.float32
    )
    grad_wdown = lax.dot_general(
        hidden_act, cot_in, (((0,), (0,)), ((), ())), preferred_element_type=jnp.float32
    )
    scores = jnp.sum(jnp.abs(grad_wgate * gate_mat.astype(jnp.float32)), axis=0)
    scores = scores + jnp.sum(jnp.abs(grad_wup * up_mat.astype(jnp.float32)), axis=0)
    scores = scores + jnp.sum(jnp.abs(grad_wdown * down_mat.astype(jnp.float32)), axis=1)
    return (hidden_act, scores)


def on_device(hidden, gain, expert_ids, gate_weights, segment_ids, upstream, w_gate, w_up, w_down):
    rows_here = hidden.shape[0]
    top_count = expert_ids.shape[1]
    experts = lax.axis_size("tok")
    groups = lax.axis_size("grp")
    capacity = 5 * rows_here // (2 * experts)
    width = w_gate.shape[1]
    documents = jnp.arange(experts * groups, dtype=jnp.int32)
    doc_onehot = (segment_ids[:, None] == documents[None, :]).astype(jnp.float32)
    doc_len = lax.psum(jnp.sum(doc_onehot, axis=0), ("tok", "grp"))
    tok_len = jnp.sum(doc_onehot * doc_len[None, :], axis=1)
    tok_weight = rows_here / tok_len
    onehot = (
        expert_ids.reshape(-1)[:, None] == jnp.arange(experts, dtype=jnp.int32)[None, :]
    ).astype(jnp.int32)
    before = jnp.cumsum(onehot, axis=0) - onehot
    slot_ids = jnp.sum(before * onehot, axis=1).reshape(rows_here, top_count)
    targets = expert_ids * capacity + slot_ids
    all_slots = jnp.arange(experts * capacity, dtype=jnp.int32)
    matches = all_slots[:, None, None] == targets[None, :, :]
    placing = jnp.any(matches, axis=2).astype(jnp.bfloat16)
    scaled = gate_weights * tok_weight[:, None]
    slot_scale = jnp.sum(jnp.where(matches, scaled[None, :, :], 0.0), axis=(1, 2))
    combining = jnp.sum(jnp.where(matches, gate_weights[None, :, :], 0.0), axis=2)
    wide_hidden = hidden.astype(jnp.float32)
    squares = lax.psum(jnp.sum(wide_hidden * wide_hidden, axis=1), "tp")
    scaling = lax.rsqrt(squares / width + 1e-05)
    normed = (wide_hidden * scaling[:, None] * gain.astype(jnp.float32)[None, :]).astype(
        jnp.bfloat16
    )
    block_rows = jnp.dot(placing, normed, preferred_element_type=jnp.float32).astype(jnp.bfloat16)
    block_cot = jnp.dot(placing, upstream, preferred_element_type=jnp.float32) * slot_scale[:, None]
    block_rows = block_rows.reshape(experts, capacity, -1)
    block_cot = block_cot.astype(jnp.bfloat16).reshape(experts, capacity, -1)
    came_rows, came_cot = (
        lax.all_to_all(block_rows, "tok", split_axis=0, concat_axis=0, tiled=True),
        lax.all_to_all(block_cot, "tok", split_axis=0, concat_axis=0, tiled=True),
    )
    part_rows, part_cot = (
        lax.all_gather(came_rows, "tp", axis=2, tiled=True),
        lax.all_gather(came_cot, "tp", axis=2, tiled=True),
    )
    pooled_rows, pooled_cot = (
        lax.all_gather(part_rows, "grp", axis=0, tiled=True),
        lax.all_gather(part_cot, "grp", axis=0, tiled=True),
    )
    rows_in = pooled_rows.reshape(-1, width)
    cot_in = pooled_cot.reshape(-1, width)
    gate_mat = w_gate[0]
    up_mat = w_up[0]
    down_mat = w_down[0]
    hidden_act, scores = expert_pass(rows_in, cot_in, gate_mat, up_mat, down_mat)
    importance = scores / (rows_here * experts * groups)
    partial_value = lax.psum_scatter(
        lax.dot_general(
            down_mat, hidden_act, (((0,), (1,)), ((), ())), preferred_element_type=jnp.float32
        ).astype(jnp.bfloat16),
        "tp",
        scatter_dimension=0,
        tiled=True,
    )
    summed = lax.psum_scatter(partial_value, "grp", scatter_dimension=1, tiled=True).astype(
        jnp.float32
    )
    slice_width = summed.shape[0]
    outgoing = summed.astype(jnp.bfloat16).reshape(slice_width, experts, capacity)
    returned = lax.all_to_all(outgoing, "tok", split_axis=1, concat_axis=1, tiled=True)
    returned = returned.reshape(slice_width, experts * capacity).astype(jnp.float32)
    combined = lax.dot_general(
        combining,
        returned,
        (((0,), (1,)), ((), ())),
        precision=lax.Precision.HIGHEST,
        preferred_element_type=jnp.float32,
    )
    mixed = (hidden.astype(jnp.float32) + combined).astype(jnp.bfloat16)
    return (mixed, importance[None, :])


def solution(mesh):
    placed = (
        P(("tok", "grp"), "tp"),
        P("tp"),
        P(("tok", "grp"), None),
        P(("tok", "grp"), None),
        P(("tok", "grp")),
        P(("tok", "grp"), "tp"),
        P("tok", None, ("tp", "grp")),
        P("tok", None, ("tp", "grp")),
        P("tok", ("tp", "grp"), None),
    )
    return jax.shard_map(
        on_device,
        mesh=mesh,
        in_specs=placed,
        out_specs=(P(("tok", "grp"), "tp"), P("tok", ("tp", "grp"))),
        check_vma=False,
    )
```

profile of v0, /device:TPU:1, one launch (start us, length us, event | category | flops | bytes accessed | tf_op | source)
XLA Modules:
  0.0 378.7 jit_solution(2218602018310981666)
XLA Ops:
  7.2 0.9 copy.31
  8.5 1.0 fusion.19
  9.5 34.2 %psum.14 = f32[128]{0:T(128)S(1)} all-reduce(f32[128]{0:T(128)S(1)} %fusion.19), channel_id=1, replica_groups=mesh['tok'=8,'tp'=16,'grp'=2] {'tp'}, use_global_device_ids=true, to_apply=%region_6.7 | all-reduce | flops 128 | bytes 1024 | tf_op jit(solution)/shard_map/psum | solution.py:60
  43.7 0.7 convert_element_type.60
  45.5 0.7 multiply_add_fusion
  46.3 1.2 convolution_convert_fusion.1
  47.5 17.2 %all_to_all.15 = bf16[8,40,384]{2,1,0:T(8,128)(2,1)} all-to-all(bf16[8,40,384]{2,1,0:T(8,128)(2,1)S(1)} %bitcast.56), channel_id=1, replica_groups=mesh['tok'=8,'tp'=16,'grp'=2] {'tok'}, dimensions={0} | all-to-all | bytes 491520 | tf_op jit(solution)/shard_map/all_to_all | solution.py:70
  64.8 0.8 convert_reduce_fusion
  65.6 32.2 %psum.15 = f32[16]{0:T(128)S(1)} all-reduce(f32[16]{0:T(128)S(1)} %convert_reduce_fusion), channel_id=1, replica_groups=mesh['tok'=8,'tp'=16,'grp'=2] {'tok','grp'}, use_global_device_ids=true, to_apply=%region_10.11 | all-reduce | flops 16 | bytes 128 | tf_op jit(solution)/shard_map/psum | solution.py:44
  97.8 0.7 select_reduce_fusion.2
  99.2 1.5 select_reduce_fusion
  101.0 12.8 %all_to_all.16 = bf16[8,40,384]{2,1,0:T(8,128)(2,1)} all-to-all(bf16[8,40,384]{2,1,0:T(8,128)(2,1)S(1)} %bitcast.57), channel_id=1, replica_groups=mesh['tok'=8,'tp'=16,'grp'=2] {'tok'}, dimensions={0} | all-to-all | bytes 491520 | tf_op jit(solution)/shard_map/all_to_all | solution.py:71
  113.8 10.2 %all-gather.5.cloned.1.call-done = bf16[8,40,6144]{2,1,0:T(8,128)(2,1)} async-done(((bf16[8,40,384]{2,1,0:T(8,128)(2,1)}), bf16[8,40,6144]{2,1,0:T(8,128)(2,1)}) %all-gather.5.cloned.1.call-update) | async-done | bytes 3932176 | tf_op jit(solution)/shard_map/all_gather | solution.py:74
  124.1 62.4 %all-gather.9.cloned.1.call-done = bf16[8,40,6144]{2,1,0:T(8,128)(2,1)} async-done(((bf16[8,40,384]{2,1,0:T(8,128)(2,1)}), bf16[8,40,6144]{2,1,0:T(8,128)(2,1)}) %all-gather.9.cloned.1.call-update) | async-done | bytes 3932176 | tf_op jit(solution)/shard_map/all_gather | solution.py:75
  186.5 27.7 %all-gather.7.cloned.1.call-done = bf16[16,40,6144]{2,1,0:T(8,128)(2,1)} async-done(((bf16[8,40,6144]{2,1,0:T(8,128)(2,1)}), bf16[16,40,6144]{2,1,0:T(8,128)(2,1)}) %all-gather.7.cloned.1.call-update) | async-done | bytes 7864336 | tf_op jit(solution)/shard_map/all_gather | solution.py:78
  214.2 5.6 %fusion.9 = f32[640,256]{1,0:T(8,128)S(1)} fusion(bf16[640,6144]{1,0:T(8,128)(2,1)} %bitcast.60, bf16[1,6144,256]{2,1,0:T(8,128)(2,1)S(1)} %copy-done.4), kind=kOutput, calls=%fused_computation.13 | convolution fusion | flops 2013265920 | bytes 11665408 | tf_op jit(solution)/shard_map/dot_general | solution.py:8
  219.8 0.8 copy-done.6
  220.6 3.0 multiply_convert_fusion.2
  223.6 0.7 copy-done.2
  224.4 6.1 %fusion = bf16[6144,640]{0,1:T(8,128)(2,1)} fusion(bf16[640,256]{1,0:T(8,128)(2,1)S(1)} %get-tuple-element.4, bf16[1,256,6144]{2,1,0:T(8,128)(2,1)S(1)} %copy-done.1), kind=kOutput, calls=%fused_computation.1 | convolution fusion | flops 2017198080 | bytes 11337728 | tf_op jit(solution)/shard_map/dot_general | solution.py:89
  230.5 10.7 %copy.34 = bf16[6144,640]{1,0:T(8,128)(2,1)} copy(bf16[6144,640]{0,1:T(8,128)(2,1)} %fusion) | data formatting | bytes 15728640
  241.6 5.6 %fusion.4 = f32[640,256]{1,0:T(8,128)S(1)} fusion(bf16[640,6144]{1,0:T(8,128)(2,1)} %bitcast.53, bf16[1,256,6144]{2,1,0:T(8,128)(2,1)S(1)} %copy-done.1), kind=kOutput, calls=%fused_computation.8 | convolution fusion | flops 2013265920 | bytes 11665408 | tf_op jit(solution)/shard_map/dot_general | solution.py:13
  247.2 0.8 copy-done.9
  248.1 6.2 %fusion.11 = f32[256]{0:T(256)S(1)} fusion(bf16[1,6144,256]{2,1,0:T(8,128)(2,1)S(1)} %copy-done.5, bf16[640,6144]{1,0:T(8,128)(2,1)} %bitcast.61, f32[640,256]{1,0:T(8,128)S(1)} %copy-done.8, f32[640,256]{1,0:T(8,128)S(1)} %fusion.4, f32[640,256]{1,0:T(8,128)S(1)} %copy-done.10), kind=kOutput, calls=%fused_computation.15 | convolution fusion | flops 2021195520 | bytes 12977152 | tf_op jit(solution)/shard_map/dot_general | solution.py:20
  254.3 80.1 %reduce-scatter.7.cloned.1.call-done = bf16[384,640]{1,0:T(8,128)(2,1)} async-done(((bf16[6144,640]{1,0:T(8,128)(2,1)}), bf16[384,640]{1,0:T(8,128)(2,1)}) %reduce-scatter.7.cloned.1.call-update) | async-done | bytes 491536
  334.4 2.0 copy.35
  336.5 7.4 %fusion.12 = f32[256]{0:T(256)S(1)} fusion(bf16[1,6144,256]{2,1,0:T(8,128)(2,1)} %param.16, bf16[640,6144]{1,0:T(8,128)(2,1)} %bitcast.62, f32[640,256]{1,0:T(8,128)} %copy-done.9, f32[640,256]{1,0:T(8,128)} %copy-done.7), kind=kOutput, calls=%fused_computation.16 | convolution fusion | flops 2020540160 | bytes 12321792 | tf_op jit(solution)/shard_map/dot_general | solution.py:23
  343.8 7.7 %reduce-scatter.5.cloned.1.call-done = bf16[384,320]{0,1:T(8,128)(2,1)} async-done(((bf16[384,640]{0,1:T(8,128)(2,1)}), bf16[384,320]{0,1:T(8,128)(2,1)}) %reduce-scatter.5.cloned.1.call-update) | async-done | bytes 245776 | tf_op jit(solution)/shard_map/reduce_scatter | solution.py:96
  351.5 6.5 %all-to-all-start.1 = ((bf16[384,8,40]{0,2,1:T(8,128)(2,1)}), bf16[384,8,40]{0,2,1:T(8,128)(2,1)S(1)}, u32[]{:S(2)}, u32[]{:S(2)}) async-start(bf16[384,8,40]{0,2,1:T(8,128)(2,1)} %bitcast.58), calls=%async_computation.2 | async-start | bytes 491520 | tf_op jit(solution)/shard_map/all_to_all | solution.py:101
  358.0 6.5 %fusion.13 = f32[256]{0:T(256)S(1)} fusion(bf16[1,256,6144]{2,1,0:T(8,128)(2,1)S(1)} %copy-done.1, bf16[640,256]{1,0:T(8,128)(2,1)} %copy-done.2, bf16[640,6144]{1,0:T(8,128)(2,1)} %bitcast.54), kind=kOutput, calls=%fused_computation.17 | convolution fusion | flops 2019557120 | bytes 11338752 | tf_op jit(solution)/shard_map/dot_general | solution.py:26
  365.0 4.8 %all-to-all-done.1 = bf16[384,8,40]{0,2,1:T(8,128)(2,1)S(1)} async-done(((bf16[384,8,40]{0,2,1:T(8,128)(2,1)}), bf16[384,8,40]{0,2,1:T(8,128)(2,1)S(1)}, u32[]{:S(2)}, u32[]{:S(2)}) %all-to-all-start.1) | async-done | bytes 245792 | tf_op jit(solution)/shard_map/all_to_all | solution.py:101
  369.8 2.0 fusion.15
  (48 shorter events, 3.6 us)
Async XLA Ops:
  7.2 93.6 %copy-start = (bf16[128,384]{1,0:T(8,128)(2,1)S(1)}, bf16[128,384]{1,0:T(8,128)(2,1)}, u32[]{:S(2)}) copy-start(bf16[128,384]{1,0:T(8,128)(2,1)} %param.14) | copy-start | bytes 294916
  7.2 207.0 %copy-start.4 = (bf16[1,6144,256]{2,1,0:T(8,128)(2,1)S(1)}, bf16[1,6144,256]{2,1,0:T(8,128)(2,1)}, u32[]{:S(2)}) copy-start(bf16[1,6144,256]{2,1,0:T(8,128)(2,1)} %param.15) | copy-start | bytes 9437188
  7.2 116.8 %all-gather.5.cloned.1.call-start = ((), (), s32[]{:S(2)}) async-start(), calls=%async_computation.5 | async-start | bytes 4177920 | tf_op jit(solution)/shard_map/all_gather | solution.py:74
  64.7 121.7 %all-gather.9.cloned.1.call-start = ((), (), s32[]{:S(2)}) async-start(), calls=%async_computation.8 | async-start | bytes 4177920 | tf_op jit(solution)/shard_map/all_gather | solution.py:75
  113.8 100.4 %all-gather.7.cloned.1.call-start = ((), (), s32[]{:S(2)}) async-start(), calls=%async_computation.6 | async-start | bytes 11796480 | tf_op jit(solution)/shard_map/all_gather | solution.py:78
  124.1 117.6 %all-gather.11.cloned.1.call-start = ((), (), s32[]{:S(2)}) async-start(), calls=%async_computation.9 | async-start | bytes 11796480 | tf_op jit(solution)/shard_map/all_gather | solution.py:79
  186.5 147.9 %reduce-scatter.7.cloned.1.call-start = ((), (), s32[]{:S(2)}) async-start(), calls=%async_computation.10 | async-start | bytes 8355840
  214.2 5.6 %copy-start.3 = (bf16[16,40,6144]{2,1,0:T(8,128)(2,1)S(1)}, bf16[16,40,6144]{2,1,0:T(8,128)(2,1)}, u32[]{:S(2)}) copy-start(bf16[16,40,6144]{2,1,0:T(8,128)(2,1)} %all-gather.7.cloned.1.call-done) | copy-start | bytes 23592964
  214.2 6.4 %copy-start.6 = (bf16[1,6144,256]{2,1,0:T(8,128)(2,1)S(1)}, bf16[1,6144,256]{2,1,0:T(8,128)(2,1)}, u32[]{:S(2)}) copy-start(bf16[1,6144,256]{2,1,0:T(8,128)(2,1)} %param.16) | copy-start | bytes 9437188
  220.6 3.0 copy-start.7
  220.6 3.8 copy-start.1
  223.6 0.7 copy-start.2
  241.2 110.2 %reduce-scatter.5.cloned.1.call-start = ((), (), s32[]{:S(2)}) async-start(), calls=%async_computation.7 | async-start | bytes 737280 | tf_op jit(solution)/shard_map/reduce_scatter | solution.py:96
  241.6 6.5 %copy-start.5 = (bf16[1,6144,256]{2,1,0:T(8,128)(2,1)S(1)}, bf16[1,6144,256]{2,1,0:T(8,128)(2,1)}, u32[]{:S(2)}) copy-start(bf16[1,6144,256]{2,1,0:T(8,128)(2,1)} %param.15) | copy-start | bytes 9437188
  241.6 6.5 %copy-start.8 = (f32[640,256]{1,0:T(8,128)S(1)}, f32[640,256]{1,0:T(8,128)}, u32[]{:S(2)}) copy-start(f32[640,256]{1,0:T(8,128)} %copy-done.7) | copy-start | bytes 1966084
  241.6 6.5 %copy-start.10 = (f32[640,256]{1,0:T(8,128)S(1)}, f32[640,256]{1,0:T(8,128)}, u32[]{:S(2)}) copy-start(f32[640,256]{1,0:T(8,128)} %get-tuple-element.5) | copy-start | bytes 1966084
  247.2 0.8 copy-start.9
  351.5 18.3 %all-to-all-start.1 = ((bf16[384,8,40]{0,2,1:T(8,128)(2,1)}), bf16[384,8,40]{0,2,1:T(8,128)(2,1)S(1)}, u32[]{:S(2)}, u32[]{:S(2)}) async-start(bf16[384,8,40]{0,2,1:T(8,128)(2,1)} %bitcast.58), calls=%async_computation.2 | async-start | bytes 491520 | tf_op jit(solution)/shard_map/all_to_all | solution.py:101
Sparse Core Ops, SparseCore 0:
  64.9 59.1 all-gather.4
  126.4 59.9 all-gather.8
  188.3 25.9 all-gather.6
  215.9 25.6 all-gather.10
  245.3 89.1 reduce-scatter.6
  336.8 14.6 reduce-scatter.4
where the time goes:
time: 379 us
  waiting for transfers between devices  193 us (51%)
  blocking collectives  96.5 us (25%)
  matrix products  43.9 us (12%)
  local copies, waits for them, and re-layouts  16.8 us (4%)
  between operations  14.2 us (4%)
  other arithmetic  7.42 us (2%)
  starting transfers between devices  6.89 us (2%)
    unnamed x7, waiting for transfers between devices  80.2 us
    all_gather x1, waiting for transfers between devices, on_device(): lax.all_gather(came_cot, 'tp', axis=2, tiled=True)  62.4 us
    psum x1, blocking collectives, on_device(): squares = lax.psum(jnp.sum(wide_hidden * wide_hidden, axis=1), 'tp')  34.2 us
    psum x1, blocking collectives, on_device(): doc_len = lax.psum(jnp.sum(doc_onehot, axis=0), ('tok', 'grp'))  32.2 us
    all_gather x1, waiting for transfers between devices, on_device(): lax.all_gather(part_rows, 'grp', axis=0, tiled=True)  27.7 us
    all_to_all x1, blocking collectives, on_device(): lax.all_to_all(block_rows, 'tok', split_axis=0, concat_axis=0, tiled=True)  17.2 us
    unnamed x25, local copies, waits for them, and re-layouts  16.1 us
    all_to_all x1, blocking collectives, on_device(): lax.all_to_all(block_cot, 'tok', split_axis=0, concat_axis=0, tiled=True)  12.8 us
  transfers between devices with their start and end apart: 7, of which 7 were waited for; matrix products, arithmetic and copies ran while one was open for 15% of the time, Pallas kernels for 0%

commit v1 on v0

--- a/solution.py
+++ b/solution.py
@@ -72,7 +72,9 @@
     )
     part_rows, part_cot = (
         lax.all_gather(came_rows, "tp", axis=2, tiled=True),
-        lax.all_gather(came_cot, "tp", axis=2, tiled=True),
+        jnp.concatenate(
+            lax.all_to_all(jnp.stack([came_cot] * lax.axis_size("tp")), "tp", 0, 0), axis=2
+        ),
     )
     pooled_rows, pooled_cot = (
         lax.all_gather(part_rows, "grp", axis=0, tiled=True),

time: 379 us -> 382 us (level)
  waiting for transfers between devices: 193 us -> 146 us
  blocking collectives: 96.5 us -> 143 us
    all_gather x1 -> x0, waiting for transfers between devices: 62.4 us -> none  [on_device(): lax.all_gather(came_cot, 'tp', axis=2, tiled=True)]
    all_to_all x0 -> x1, blocking collectives: none -> 50.3 us  [on_device(): lax.all_to_all(jnp.stack([came_cot] * lax.axis_size('tp')), 'tp', 0, 0)]
    all_gather x1, waiting for transfers between devices: 10.2 us -> 59.2 us  [on_device(): lax.all_gather(came_rows, 'tp', axis=2, tiled=True)]
    all_gather x1, waiting for transfers between devices: 27.7 us -> 0.02 us  [on_device(): lax.all_gather(part_rows, 'grp', axis=0, tiled=True)]
    psum x1, blocking collectives: 32.2 us -> 25.4 us  [on_device(): doc_len = lax.psum(jnp.sum(doc_onehot, axis=0), ('tok', 'grp'))]
    unnamed x7 -> x6, waiting for transfers between devices: 80.2 us -> 74.1 us
  transfers between devices with their start and end apart: 7 -> 6, of which waited for: 7 -> 4; matrix products, arithmetic and copies ran while one was open for 15% -> 16% of each run, Pallas kernels for 0% -> 0%
where the time goes in v1:
time: 382 us; the launch traced here: 381 us
  waiting for transfers between devices  146 us (38%)
  blocking collectives  143 us (37%)
  matrix products  44.1 us (12%)
  local copies, waits for them, and re-layouts  19.9 us (5%)
  between operations  13.9 us (4%)
  other arithmetic  7.42 us (2%)
  starting transfers between devices  6.86 us (2%)
    unnamed x6, waiting for transfers between devices  74.1 us
    all_gather x1, waiting for transfers between devices, on_device(): lax.all_gather(came_rows, 'tp', axis=2, tiled=True)  59.2 us
    all_to_all x1, blocking collectives, on_device(): lax.all_to_all(jnp.stack([came_cot] * lax.axis_size('tp')), 'tp', 0, 0)  50.3 us
    psum x1, blocking collectives, on_device(): squares = lax.psum(jnp.sum(wide_hidden * wide_hidden, axis=1), 'tp')  34.2 us
    psum x1, blocking collectives, on_device(): doc_len = lax.psum(jnp.sum(doc_onehot, axis=0), ('tok', 'grp'))  25.4 us
    all_to_all x1, blocking collectives, on_device(): lax.all_to_all(block_rows, 'tok', split_axis=0, concat_axis=0, tiled=True)  17.2 us
    all_to_all x1, blocking collectives, on_device(): lax.all_to_all(block_cot, 'tok', split_axis=0, concat_axis=0, tiled=True)  16.1 us
    unnamed x25, local copies, waits for them, and re-layouts  16 us
  transfers between devices with their start and end apart: 6, of which 4 were waited for; matrix products, arithmetic and copies ran while one was open for 16% of the time, Pallas kernels for 0%

profile of v1, /device:TPU:1, one launch (start us, length us, event | category | flops | bytes accessed | tf_op | source)
XLA Modules:
  0.0 381.4 jit_solution(1369163450564881255)
XLA Ops:
  7.2 0.8 copy.33
  8.3 1.0 fusion.19
  9.3 34.2 %psum.14 = f32[128]{0:T(128)S(1)} all-reduce(f32[128]{0:T(128)S(1)} %fusion.19), channel_id=1, replica_groups=mesh['tok'=8,'tp'=16,'grp'=2] {'tp'}, use_global_device_ids=true, to_apply=%region_6.7 | all-reduce | flops 128 | bytes 1024 | tf_op jit(solution)/shard_map/psum | solution.py:60
  45.4 0.7 multiply_add_fusion
  46.1 1.2 convolution_convert_fusion.1
  47.3 17.2 %all_to_all.20 = bf16[8,40,384]{2,1,0:T(8,128)(2,1)} all-to-all(bf16[8,40,384]{2,1,0:T(8,128)(2,1)S(1)} %bitcast.61), channel_id=1, replica_groups=mesh['tok'=8,'tp'=16,'grp'=2] {'tok'}, dimensions={0} | all-to-all | bytes 491520 | tf_op jit(solution)/shard_map/all_to_all | solution.py:70
  64.6 59.2 %all-gather.4.cloned.1.call-done = bf16[8,40,6144]{2,1,0:T(8,128)(2,1)} async-done(((bf16[8,40,384]{2,1,0:T(8,128)(2,1)}), bf16[8,40,6144]{2,1,0:T(8,128)(2,1)}) %all-gather.4.cloned.1.call-update) | async-done | bytes 3932176 | tf_op jit(solution)/shard_map/all_gather | solution.py:74
  123.9 0.8 convert_reduce_fusion
  124.7 25.4 %psum.15 = f32[16]{0:T(128)S(1)} all-reduce(f32[16]{0:T(128)S(1)} %convert_reduce_fusion), channel_id=1, replica_groups=mesh['tok'=8,'tp'=16,'grp'=2] {'tok','grp'}, use_global_device_ids=true, to_apply=%region_10.11 | all-reduce | flops 16 | bytes 128 | tf_op jit(solution)/shard_map/psum | solution.py:44
  150.1 0.7 select_reduce_fusion.2
  150.9 0.7 broadcast_multiply_fusion
  151.6 1.5 select_reduce_fusion
  153.3 16.1 %all_to_all.21 = bf16[8,40,384]{2,1,0:T(8,128)(2,1)S(1)} all-to-all(bf16[8,40,384]{2,1,0:T(8,128)(2,1)S(1)} %bitcast.62), channel_id=1, replica_groups=mesh['tok'=8,'tp'=16,'grp'=2] {'tok'}, dimensions={0} | all-to-all | bytes 491520 | tf_op jit(solution)/shard_map/all_to_all | solution.py:71
  170.0 50.3 %all_to_all.22 = bf16[16,8,40,384]{3,2,1,0:T(8,128)(2,1)S(1)} all-to-all(bf16[16,8,40,384]{3,2,1,0:T(8,128)(2,1)S(1)} %stack.2), channel_id=1, replica_groups=mesh['tok'=8,'tp'=16,'grp'=2] {'tp'}, dimensions={0} | all-to-all | bytes 7864320 | tf_op jit(solution)/shard_map/all_to_all | solution.py:76
  220.3 2.6 copy.39
  223.0 5.6 %fusion.9 = f32[640,256]{1,0:T(8,128)S(1)} fusion(bf16[640,6144]{1,0:T(8,128)(2,1)} %bitcast.65, bf16[1,6144,256]{2,1,0:T(8,128)(2,1)S(1)} %copy-done.4), kind=kOutput, calls=%fused_computation.13 | convolution fusion | flops 2013265920 | bytes 11665408 | tf_op jit(solution)/shard_map/dot_general | solution.py:8
  228.6 0.8 copy-done.6
  229.4 3.0 multiply_convert_fusion.2
  232.4 0.7 copy-done.2
  233.1 6.4 %fusion = bf16[6144,640]{0,1:T(8,128)(2,1)} fusion(bf16[640,256]{1,0:T(8,128)(2,1)S(1)} %get-tuple-element.4, bf16[1,256,6144]{2,1,0:T(8,128)(2,1)S(1)} %copy-done.1), kind=kOutput, calls=%fused_computation.1 | convolution fusion | flops 2017198080 | bytes 11337728 | tf_op jit(solution)/shard_map/dot_general | solution.py:91
  239.5 10.9 %copy.37 = bf16[6144,640]{1,0:T(8,128)(2,1)} copy(bf16[6144,640]{0,1:T(8,128)(2,1)} %fusion) | data formatting | bytes 15728640
  250.7 5.6 %fusion.4 = f32[640,256]{1,0:T(8,128)S(1)} fusion(bf16[640,6144]{1,0:T(8,128)(2,1)} %bitcast.58, bf16[1,256,6144]{2,1,0:T(8,128)(2,1)S(1)} %copy-done.1), kind=kOutput, calls=%fused_computation.8 | convolution fusion | flops 2013265920 | bytes 11665408 | tf_op jit(solution)/shard_map/dot_general | solution.py:13
  256.3 0.8 copy-done.9
  257.1 6.2 %fusion.11 = f32[256]{0:T(256)S(1)} fusion(bf16[1,6144,256]{2,1,0:T(8,128)(2,1)S(1)} %copy-done.5, bf16[640,6144]{1,0:T(8,128)(2,1)} %bitcast.66, f32[640,256]{1,0:T(8,128)S(1)} %copy-done.8, f32[640,256]{1,0:T(8,128)S(1)} %fusion.4, f32[640,256]{1,0:T(8,128)S(1)} %copy-done.10), kind=kOutput, calls=%fused_computation.15 | convolution fusion | flops 2021195520 | bytes 12977152 | tf_op jit(solution)/shard_map/dot_general | solution.py:20
  263.4 74.0 %reduce-scatter.7.cloned.1.call-done = bf16[384,640]{1,0:T(8,128)(2,1)} async-done(((bf16[6144,640]{1,0:T(8,128)(2,1)}), bf16[384,640]{1,0:T(8,128)(2,1)}) %reduce-scatter.7.cloned.1.call-update) | async-done | bytes 491536
  337.4 2.0 copy.38
  339.4 7.4 %fusion.12 = f32[256]{0:T(256)S(1)} fusion(bf16[1,6144,256]{2,1,0:T(8,128)(2,1)} %param.16, bf16[640,6144]{1,0:T(8,128)(2,1)} %bitcast.67, f32[640,256]{1,0:T(8,128)} %copy-done.9, f32[640,256]{1,0:T(8,128)} %copy-done.7), kind=kOutput, calls=%fused_computation.16 | convolution fusion | flops 2020540160 | bytes 12321792 | tf_op jit(solution)/shard_map/dot_general | solution.py:23
  346.8 7.7 %reduce-scatter.5.cloned.1.call-done = bf16[384,320]{0,1:T(8,128)(2,1)} async-done(((bf16[384,640]{0,1:T(8,128)(2,1)}), bf16[384,320]{0,1:T(8,128)(2,1)}) %reduce-scatter.5.cloned.1.call-update) | async-done | bytes 245776 | tf_op jit(solution)/shard_map/reduce_scatter | solution.py:98
  354.5 6.5 %all-to-all-start.1 = ((bf16[384,8,40]{0,2,1:T(8,128)(2,1)}), bf16[384,8,40]{0,2,1:T(8,128)(2,1)S(1)}, u32[]{:S(2)}, u32[]{:S(2)}) async-start(bf16[384,8,40]{0,2,1:T(8,128)(2,1)} %bitcast.63), calls=%async_computation.2 | async-start | bytes 491520 | tf_op jit(solution)/shard_map/all_to_all | solution.py:103
  361.0 6.5 %fusion.13 = f32[256]{0:T(256)S(1)} fusion(bf16[1,256,6144]{2,1,0:T(8,128)(2,1)S(1)} %copy-done.1, bf16[640,256]{1,0:T(8,128)(2,1)} %copy-done.2, bf16[640,6144]{1,0:T(8,128)(2,1)} %bitcast.59), kind=kOutput, calls=%fused_computation.17 | convolution fusion | flops 2019557120 | bytes 11338752 | tf_op jit(solution)/shard_map/dot_general | solution.py:26
  368.0 4.8 %all-to-all-done.1 = bf16[384,8,40]{0,2,1:T(8,128)(2,1)S(1)} async-done(((bf16[384,8,40]{0,2,1:T(8,128)(2,1)}), bf16[384,8,40]{0,2,1:T(8,128)(2,1)S(1)}, u32[]{:S(2)}, u32[]{:S(2)}) %all-to-all-start.1) | async-done | bytes 245792 | tf_op jit(solution)/shard_map/all_to_all | solution.py:103
  372.8 2.0 fusion.15
  (48 shorter events, 4.1 us)
Async XLA Ops:
  7.2 145.9 %copy-start = (bf16[128,384]{1,0:T(8,128)(2,1)S(1)}, bf16[128,384]{1,0:T(8,128)(2,1)}, u32[]{:S(2)}) copy-start(bf16[128,384]{1,0:T(8,128)(2,1)} %param.14) | copy-start | bytes 294916
  7.2 116.7 %all-gather.4.cloned.1.call-start = ((), (), s32[]{:S(2)}) async-start(), calls=%async_computation.6 | async-start | bytes 4177920 | tf_op jit(solution)/shard_map/all_gather | solution.py:74
  64.6 158.4 %all-gather.6.cloned.1.call-start = ((), (), s32[]{:S(2)}) async-start(), calls=%async_computation.7 | async-start | bytes 11796480 | tf_op jit(solution)/shard_map/all_gather | solution.py:80
  123.9 126.7 %all-gather.8.cloned.1.call-start = ((), (), s32[]{:S(2)}) async-start(), calls=%async_computation.9 | async-start | bytes 11796480 | tf_op jit(solution)/shard_map/all_gather | solution.py:81
  220.3 2.7 copy-start.4
  222.9 114.5 %reduce-scatter.7.cloned.1.call-start = ((), (), s32[]{:S(2)}) async-start(), calls=%async_computation.10 | async-start | bytes 8355840
  223.0 5.6 %copy-start.3 = (bf16[16,40,6144]{2,1,0:T(8,128)(2,1)S(1)}, bf16[16,40,6144]{2,1,0:T(8,128)(2,1)}, u32[]{:S(2)}) copy-start(bf16[16,40,6144]{2,1,0:T(8,128)(2,1)} %all-gather.6.cloned.1.call-done) | copy-start | bytes 23592964
  223.0 6.4 %copy-start.6 = (bf16[1,6144,256]{2,1,0:T(8,128)(2,1)S(1)}, bf16[1,6144,256]{2,1,0:T(8,128)(2,1)}, u32[]{:S(2)}) copy-start(bf16[1,6144,256]{2,1,0:T(8,128)(2,1)} %param.16) | copy-start | bytes 9437188
  229.4 3.0 copy-start.7
  229.4 3.8 copy-start.1
  232.4 0.7 copy-start.2
  250.4 104.1 %reduce-scatter.5.cloned.1.call-start = ((), (), s32[]{:S(2)}) async-start(), calls=%async_computation.8 | async-start | bytes 737280 | tf_op jit(solution)/shard_map/reduce_scatter | solution.py:98
  250.6 6.5 %copy-start.5 = (bf16[1,6144,256]{2,1,0:T(8,128)(2,1)S(1)}, bf16[1,6144,256]{2,1,0:T(8,128)(2,1)}, u32[]{:S(2)}) copy-start(bf16[1,6144,256]{2,1,0:T(8,128)(2,1)} %param.15) | copy-start | bytes 9437188
  250.6 6.5 %copy-start.8 = (f32[640,256]{1,0:T(8,128)S(1)}, f32[640,256]{1,0:T(8,128)}, u32[]{:S(2)}) copy-start(f32[640,256]{1,0:T(8,128)} %copy-done.7) | copy-start | bytes 1966084
  250.7 6.5 %copy-start.10 = (f32[640,256]{1,0:T(8,128)S(1)}, f32[640,256]{1,0:T(8,128)}, u32[]{:S(2)}) copy-start(f32[640,256]{1,0:T(8,128)} %get-tuple-element.5) | copy-start | bytes 1966084
  256.3 0.8 copy-start.9
  354.5 18.3 %all-to-all-start.1 = ((bf16[384,8,40]{0,2,1:T(8,128)(2,1)}), bf16[384,8,40]{0,2,1:T(8,128)(2,1)S(1)}, u32[]{:S(2)}, u32[]{:S(2)}) async-start(bf16[384,8,40]{0,2,1:T(8,128)(2,1)} %bitcast.63), calls=%async_computation.2 | async-start | bytes 491520 | tf_op jit(solution)/shard_map/all_to_all | solution.py:103
Sparse Core Ops, SparseCore 0:
  64.7 59.1 all-gather.3
  125.7 25.9 all-gather.5
  223.0 21.3 all-gather.7
  250.5 86.8 reduce-scatter.6
  339.8 14.6 reduce-scatter.4
